TPU v7x, 128 devices: a whole 4x4x4 slice. The times are simulated.
128 devices in a mesh: outer: 8 (over y, core), inner: 16 (over z, x).
Axes of the slice: x: 4, y: 4, z: 4, core: 2. Of those that a mesh axis runs over, the one named last changes fastest.
Arguments:
- layer_input: bfloat16 [16384, 7168], P(('outer', 'inner')), may hold values from -6 to 6
- out_grad: bfloat16 [16384, 7168], P(('outer', 'inner')), may hold values from -3 to 3
- expert_ids: int32 [16384, 8], P(('outer', 'inner')), may hold values from 0 to 255, as said below
- route_scales: float32 [16384, 8], P(('outer', 'inner')), may hold values from 0.25 to 2.5
- w_gate: bfloat16 [8, 7168, 2048], P('outer', None, 'inner'), may hold values from -0.0625 to 0.0625
- w_up: bfloat16 [8, 7168, 2048], P('outer', None, 'inner'), may hold values from -0.0625 to 0.0625
- w_down: bfloat16 [8, 2048, 7168], P('outer', 'inner'), may hold values from -0.125 to 0.125
Outputs:
- in_grad: bfloat16 [16384, 7168], P(('outer', 'inner'))
- grad_w_gate: float32 [8, 7168, 2048], P('outer', None, 'inner')
- grad_w_up: float32 [8, 7168, 2048], P('outer', None, 'inner')
- grad_w_down: float32 [8, 2048, 7168], P('outer', 'inner')
Inputs may be any that keep to these rules, and one draw needn't show every extreme that they name: `expert_ids`: each row names 8 different experts. In each device's aligned block of 128 rows at most 6 rows name any one expert below 8, and in every draw one expert below 8 is named by exactly 6 rows of every block.
All inputs are finite; a program needn't handle non-finite values.
Results may differ from a plain program's by a relative error of at most 0.014.
Values may be sent and summed in bfloat16 or wider, within the bound.
A program may use at most 192 MiB of HBM per device.

v0:
```python
import jax
import jax.numpy as jnp
from jax import lax
from jax.sharding import PartitionSpec as P

CAP = 6


def shards(layer_input, out_grad, expert_ids, route_scales, w_gate, w_up, w_down):
    tok_count = layer_input.shape[0]
    model_width = layer_input.shape[1]
    n_outer = lax.axis_size("outer")
    top_count = expert_ids.shape[1]
    slot_count = n_outer * CAP
    route_ids = expert_ids.reshape(-1)
    onehot = (route_ids[:, None] == jnp.arange(n_outer, dtype=jnp.int32)[None, :]).astype(jnp.int32)
    position = jnp.sum((jnp.cumsum(onehot, axis=0) - onehot) * onehot, axis=1)
    slot = jnp.where(route_ids < n_outer, route_ids * CAP + position, -1)
    picks = slot[:, None] == jnp.arange(slot_count, dtype=jnp.int32)[None, :]
    place = jnp.any(picks.reshape(tok_count, top_count, slot_count), axis=1).astype(jnp.bfloat16)
    slot_scale = jnp.sum(jnp.where(picks, route_scales.reshape(-1)[:, None], 0.0), axis=0)
    take_rows = (((0,), (0,)), ((), ()))
    send_x = lax.dot_general(
        place, layer_input, take_rows, preferred_element_type=jnp.float32
    ).astype(jnp.bfloat16)
    send_dy = lax.dot_general(place, out_grad, take_rows, preferred_element_type=jnp.float32)
    routed = (send_dy * slot_scale[:, None]).astype(jnp.bfloat16)
    send_x = send_x.reshape(n_outer, CAP, model_width)
    routed = routed.reshape(n_outer, CAP, model_width)
    gate_w = w_gate[0]
    up_w = w_up[0]
    down_w = w_down[0]
    got_x, got_gy = (
        lax.all_to_all(send_x, "outer", split_axis=0, concat_axis=0, tiled=True),
        lax.all_to_all(routed, "outer", split_axis=0, concat_axis=0, tiled=True),
    )
    rows_x = lax.all_gather(got_x.reshape(-1, model_width), "inner", axis=0, tiled=True)
    rows_gy = lax.all_gather(got_gy.reshape(-1, model_width), "inner", axis=0, tiled=True)
    gate = jnp.dot(rows_x, gate_w, preferred_element_type=jnp.float32)
    up_val = jnp.dot(rows_x, up_w, preferred_element_type=jnp.float32)
    sigmoid_gate = jax.nn.sigmoid(gate)
    silu_gate = gate * sigmoid_gate
    act = (silu_gate * up_val).astype(jnp.bfloat16)
    hid_grad = lax.dot_general(
        rows_gy, down_w, (((1,), (1,)), ((), ())), preferred_element_type=jnp.float32
    )
    gate_grad = (hid_grad * up_val * sigmoid_gate * (1.0 + gate * (1.0 - sigmoid_gate))).astype(
        jnp.bfloat16
    )
    up_grad = (hid_grad * silu_gate).astype(jnp.bfloat16)
    gate_sum = lax.dot_general(rows_x, gate_grad, take_rows, preferred_element_type=jnp.float32)
    up_sum = lax.dot_general(rows_x, up_grad, take_rows, preferred_element_type=jnp.float32)
    down_sum = lax.dot_general(act, rows_gy, take_rows, preferred_element_type=jnp.float32)
    gate_store = gate_grad
    up_store = up_grad
    carry = (gate_sum, up_sum, down_sum, gate_store, up_store)
    grad_gate, grad_up, grad_down, gate_store, up_store = carry
    term = lax.dot_general(
        gate_store, gate_w, (((1,), (1,)), ((), ())), preferred_element_type=jnp.float32
    )
    mine = lax.psum_scatter(
        (
            term
            + lax.dot_general(
                up_store, up_w, (((1,), (1,)), ((), ())), preferred_element_type=jnp.float32
            )
        ).astype(jnp.bfloat16),
        "inner",
        scatter_dimension=0,
        tiled=True,
    ).astype(jnp.float32)
    mine = mine.astype(jnp.bfloat16).reshape(n_outer, CAP, model_width)
    back = lax.all_to_all(mine, "outer", split_axis=0, concat_axis=0, tiled=True).reshape(
        slot_count, model_width
    )
    in_grad = jnp.dot(place, back, preferred_element_type=jnp.float32).astype(jnp.bfloat16)
    return (in_grad, grad_gate[None], grad_up[None], grad_down[None])


def solution(mesh):
    return jax.shard_map(
        shards,
        mesh=mesh,
        in_specs=(
            P(("outer", "inner"), None),
            P(("outer", "inner"), None),
            P(("outer", "inner"), None),
            P(("outer", "inner"), None),
            P("outer", None, "inner"),
            P("outer", None, "inner"),
            P("outer", "inner", None),
        ),
        out_specs=(
            P(("outer", "inner"), None),
            P("outer", None, "inner"),
            P("outer", None, "inner"),
            P("outer", "inner", None),
        ),
        check_vma=False,
    )
```

profile of v0, /device:TPU:1, one launch (start us, length us, event | category | flops | bytes accessed | tf_op | source)
XLA Modules:
  0.0 355.3 jit_solution(1478537319193128124)
XLA Ops:
  7.2 0.0 copy-start
  7.2 0.0 all-gather.5.cloned.1.call-start
  7.2 0.9 copy.27
  8.1 0.1 eq.45
  8.2 0.1 eq.49
  8.3 2.3 reduce-window.6
  10.6 0.3 slice_reduce_fusion
  10.9 0.2 reduce-window.9
  11.1 0.1 add_bitcast_fusion
  11.2 0.1 reduce_sum.21
  11.3 0.7 add_select_fusion.1
  12.0 0.0 copy-start.4
  12.1 1.9 convolution_convert_fusion.1
  14.0 0.2 reshape.72
  14.2 19.7 %all_to_all.15 = bf16[8,6,7168]{2,1,0:T(8,128)(2,1)} all-to-all(bf16[8,6,7168]{2,1,0:T(8,128)(2,1)S(1)} %reshape.72), channel_id=1, replica_groups=mesh['outer'=8,'inner'=16] {'outer'}, dimensions={0} | all-to-all | bytes 1376256 | tf_op jit(solution)/shard_map/all_to_all | solution.py:34
  33.9 2.3 reshape.73
  36.2 0.0 all-gather.5.cloned.1.call-update
  36.2 0.0 all-gather.3.cloned.1.call-start
  36.2 0.0 copy-done.4
  36.2 0.1 copy.30
  36.3 0.1 broadcast_in_dim.35
  36.4 0.1 select_reduce_fusion
  36.6 1.9 fusion
  38.5 0.2 reshape.70
  38.7 17.8 %all_to_all.16 = bf16[8,6,7168]{2,1,0:T(8,128)(2,1)} all-to-all(bf16[8,6,7168]{2,1,0:T(8,128)(2,1)S(1)} %reshape.70), channel_id=1, replica_groups=mesh['outer'=8,'inner'=16] {'outer'}, dimensions={0} | all-to-all | bytes 1376256 | tf_op jit(solution)/shard_map/all_to_all | solution.py:35
  56.5 2.3 reshape.71
  58.7 0.0 all-gather.3.cloned.1.call-update
  58.8 0.0 reduce-scatter.2.cloned.1.call-start
  58.8 61.0 %all-gather.5.cloned.1.call-done = bf16[768,7168]{1,0:T(8,128)(2,1)} async-done(((bf16[48,7168]{1,0:T(8,128)(2,1)}), bf16[768,7168]{1,0:T(8,128)(2,1)}) %all-gather.5.cloned.1.call-update) | async-done | bytes 11010064 | tf_op jit(solution)/shard_map/all_gather | solution.py:37
  119.8 0.0 copy-done
  119.8 0.0 copy-start.2
  119.8 0.0 copy-start.3
  119.8 7.2 %fusion.3 = f32[768,128]{1,0:T(8,128)S(1)} fusion(bf16[768,7168]{1,0:T(8,128)(2,1)} %all-gather.5.cloned.1.call-done, bf16[1,7168,128]{2,1,0:T(8,128)(2,1)S(1)} %copy-done), kind=kOutput, calls=%fused_computation.10 | convolution fusion | flops 1409286144 | bytes 13238272 | tf_op jit(solution)/shard_map/dot_general | solution.py:39
  127.0 0.1 copy-done.2
  127.1 0.5 copy-done.3
  127.6 3.0 fusion.6
  130.6 74.4 %all-gather.3.cloned.1.call-done = bf16[768,7168]{1,0:T(8,128)(2,1)} async-done(((bf16[48,7168]{1,0:T(8,128)(2,1)}), bf16[768,7168]{1,0:T(8,128)(2,1)}) %all-gather.3.cloned.1.call-update) | async-done | bytes 11010064 | tf_op jit(solution)/shard_map/all_gather | solution.py:38
  205.0 7.6 %multiply_convert_fusion.1 = (bf16[768,128]{1,0:T(8,128)(2,1)S(1)}, bf16[768,128]{1,0:T(8,128)(2,1)S(1)}) fusion(f32[768,128]{1,0:T(8,128)S(1)} %fusion.3, f32[768,128]{1,0:T(8,128)S(1)} %fusion.6, bf16[768,7168]{1,0:T(8,128)(2,1)} %all-gather.3.cloned.1.call-done, bf16[1,128,7168]{2,1,0:T(8,128)(2,1)} %param.13), kind=kOutput, calls=%fused_computation.18 | convolution fusion | flops 1410564096 | bytes 14024704 | tf_op jit(solution)/shard_map/dot_general | solution.py:44
  212.7 9.0 %fusion.1 = f32[768,7168]{1,0:T(8,128)} fusion(bf16[768,128]{1,0:T(8,128)(2,1)S(1)} %get-tuple-element.5, bf16[1,7168,128]{2,1,0:T(8,128)(2,1)S(1)} %copy-done), kind=kOutput, calls=%fused_computation.8 | convolution fusion | flops 1409286144 | bytes 24051712 | tf_op jit(solution)/shard_map/dot_general | solution.py:58
  221.7 13.2 %add_convert_fusion = bf16[768,7168]{1,0:T(8,128)(2,1)} fusion(f32[768,7168]{1,0:T(8,128)} %fusion.1, bf16[768,128]{1,0:T(8,128)(2,1)S(1)} %get-tuple-element.4, bf16[1,7168,128]{2,1,0:T(8,128)(2,1)} %param.12), kind=kOutput, calls=%fused_computation | convolution fusion | flops 1420296192 | bytes 35061760 | tf_op jit(solution)/shard_map/dot_general | solution.py:64
  234.9 0.0 reduce-scatter.2.cloned.1.call-update
  234.9 9.0 %convolution_bitcast_fusion.1 = f32[1,7168,128]{2,1,0:T(8,128)} fusion(bf16[768,7168]{1,0:T(8,128)(2,1)} %all-gather.5.cloned.1.call-done, bf16[768,128]{1,0:T(8,128)(2,1)S(1)} %get-tuple-element.4), kind=kOutput, calls=%fused_computation.2 | convolution fusion | flops 1409286144 | bytes 14876672 | tf_op jit(solution)/shard_map/dot_general | solution.py:52
  243.9 9.2 %convolution_bitcast_fusion.2 = f32[1,7168,128]{2,1,0:T(8,128)} fusion(bf16[768,7168]{1,0:T(8,128)(2,1)} %all-gather.5.cloned.1.call-done, bf16[768,128]{1,0:T(8,128)(2,1)S(1)} %get-tuple-element.5), kind=kOutput, calls=%fused_computation.3 | convolution fusion | flops 1409286144 | bytes 14876672 | tf_op jit(solution)/shard_map/dot_general | solution.py:51
  253.1 72.1 %reduce-scatter.2.cloned.1.call-done = bf16[48,7168]{1,0:T(8,128)(2,1)} async-done(((bf16[768,7168]{1,0:T(8,128)(2,1)}), bf16[48,7168]{1,0:T(8,128)(2,1)}) %reduce-scatter.2.cloned.1.call-update) | async-done | bytes 688144 | tf_op jit(solution)/shard_map/reduce_scatter | solution.py:61
  325.1 2.3 reshape.74
  327.4 5.5 %all-to-all-start.2 = ((bf16[8,6,7168]{2,1,0:T(8,128)(2,1)}), bf16[8,6,7168]{2,1,0:T(8,128)(2,1)S(1)}, u32[]{:S(2)}, u32[]{:S(2)}) async-start(bf16[8,6,7168]{2,1,0:T(8,128)(2,1)} %reshape.74), calls=%async_computation.3 | async-start | bytes 1835008 | tf_op jit(solution)/shard_map/all_to_all | solution.py:73
  332.9 0.0 copy-start.1
  332.9 7.8 %convolution_bitcast_fusion = f32[1,128,7168]{2,1,0:T(8,128)} fusion(bf16[768,7168]{1,0:T(8,128)(2,1)} %all-gather.3.cloned.1.call-done, f32[768,128]{1,0:T(8,128)S(1)} %fusion.6, f32[768,128]{1,0:T(8,128)S(1)} %fusion.3), kind=kOutput, calls=%fused_computation.1 | convolution fusion | flops 1409875968 | bytes 15466496 | tf_op jit(solution)/shard_map/dot_general | solution.py:53
  340.7 5.9 %all-to-all-done.2 = bf16[8,6,7168]{2,1,0:T(8,128)(2,1)S(1)} async-done(((bf16[8,6,7168]{2,1,0:T(8,128)(2,1)}), bf16[8,6,7168]{2,1,0:T(8,128)(2,1)S(1)}, u32[]{:S(2)}, u32[]{:S(2)}) %all-to-all-start.2) | async-done | bytes 688160 | tf_op jit(solution)/shard_map/all_to_all | solution.py:73
  346.6 0.3 reshape.75
  346.8 1.9 convolution_convert_fusion
  348.7 0.0 copy-done.1
  (5 shorter events, 0.1 us)
Async XLA Ops:
  7.2 112.6 %copy-start = (bf16[1,7168,128]{2,1,0:T(8,128)(2,1)S(1)}, bf16[1,7168,128]{2,1,0:T(8,128)(2,1)}, u32[]{:S(2)}) copy-start(bf16[1,7168,128]{2,1,0:T(8,128)(2,1)} %param.11) | copy-start | bytes 5505028
  7.2 112.6 %all-gather.5.cloned.1.call-start = ((), (), s32[]{:S(2)}) async-start(), calls=%async_computation.5 | async-start | bytes 11698176 | tf_op jit(solution)/shard_map/all_gather | solution.py:37
  12.0 24.2 %copy-start.4 = (f32[128,8]{0,1:T(8,128)S(1)}, f32[128,8]{0,1:T(8,128)}, u32[]{:S(2)}) copy-start(f32[128,8]{0,1:T(8,128)} %param.10) | copy-start | bytes 12292
  36.2 168.8 %all-gather.3.cloned.1.call-start = ((), (), s32[]{:S(2)}) async-start(), calls=%async_computation.4 | async-start | bytes 11698176 | tf_op jit(solution)/shard_map/all_gather | solution.py:38
  58.8 266.4 %reduce-scatter.2.cloned.1.call-start = ((), (), s32[]{:S(2)}) async-start(), calls=%async_computation.6 | async-start | bytes 11698176 | tf_op jit(solution)/shard_map/reduce_scatter | solution.py:61
  119.8 7.3 %copy-start.2 = (bf16[768,7168]{1,0:T(8,128)(2,1)S(1)}, bf16[768,7168]{1,0:T(8,128)(2,1)}, u32[]{:S(2)}) copy-start(bf16[768,7168]{1,0:T(8,128)(2,1)} %all-gather.5.cloned.1.call-done) | copy-start | bytes 33030148
  119.8 7.8 %copy-start.3 = (bf16[1,7168,128]{2,1,0:T(8,128)(2,1)S(1)}, bf16[1,7168,128]{2,1,0:T(8,128)(2,1)}, u32[]{:S(2)}) copy-start(bf16[1,7168,128]{2,1,0:T(8,128)(2,1)} %param.12) | copy-start | bytes 5505028
  327.4 19.2 %all-to-all-start.2 = ((bf16[8,6,7168]{2,1,0:T(8,128)(2,1)}), bf16[8,6,7168]{2,1,0:T(8,128)(2,1)S(1)}, u32[]{:S(2)}, u32[]{:S(2)}) async-start(bf16[8,6,7168]{2,1,0:T(8,128)(2,1)} %reshape.74), calls=%async_computation.3 | async-start | bytes 1835008 | tf_op jit(solution)/shard_map/all_to_all | solution.py:73
  332.9 15.9 %copy-start.1 = (bf16[1,7168,128]{2,1,0:T(8,128)(2,1)S(1)}, bf16[1,7168,128]{2,1,0:T(8,128)(2,1)}, u32[]{:S(2)}) copy-start(bf16[1,7168,128]{2,1,0:T(8,128)(2,1)} %param.11) | copy-start | bytes 5505028
Sparse Core Ops, SparseCore 0:
  36.3 83.4 all-gather.4
  122.5 82.4 all-gather.2
  235.0 90.0 reduce-scatter.1
where the time goes:
time: 356 us; the launch traced here: 355 us
  waiting for transfers between devices  213 us (60%)
  matrix products  71.7 us (20%)
  blocking collectives  37.4 us (11%)
  between operations  13.9 us (4%)
  local copies, waits for them, and re-layouts  9.88 us (3%)
  starting transfers between devices  5.58 us (2%)
    all_gather x1, waiting for transfers between devices, shards(): lax.all_gather(got_gy.reshape(-1, model_width), 'inner', axis=0, tiled=True)  74.4 us
    reduce_scatter x1, waiting for transfers between devices, shards(): lax.psum_scatter((term + lax.dot_general(up_store, up_w, (((1,), (1,)), (...  72.1 us
    all_gather x1, waiting for transfers between devices, shards(): lax.all_gather(got_x.reshape(-1, model_width), 'inner', axis=0, tiled=True)  61 us
    all_to_all x1, blocking collectives, shards(): lax.all_to_all(send_x, 'outer', split_axis=0, concat_axis=0, tiled=True)  19.7 us
    all_to_all x1, blocking collectives, shards(): lax.all_to_all(routed, 'outer', split_axis=0, concat_axis=0, tiled=True)  17.8 us
    dot_general x1, matrix products, shards(): lax.dot_general(up_store, up_w, (((1,), (1,)), ((), ())), preferred_eleme...  13.2 us
    dot_general x1, matrix products, shards(): lax.dot_general(rows_x, gate_grad, take_rows, preferred_element_type=jnp....  9.15 us
    dot_general x1, matrix products, shards(): lax.dot_general(rows_x, up_grad, take_rows, preferred_element_type=jnp.fl...  9.03 us
  transfers between devices with their start and end apart: 4, of which 4 were waited for; matrix products, arithmetic and copies ran while one was open for 12% of the time, Pallas kernels for 0%

commit v1 on v0

v1 whole, which is shorter than its diff:
```python
import jax
import jax.numpy as jnp
from jax import lax
from jax.experimental import pallas as pl
from jax.experimental.pallas import tpu as pltpu
from jax.sharding import PartitionSpec as P

CAP = 6
PAD = 8
SIDE = 4
BF = jnp.bfloat16
F32 = jnp.float32
MESH = pl.DeviceIdType.MESH
NN = (((1,), (0,)), ((), ()))
NT = (((1,), (1,)), ((), ()))
TN = (((0,), (0,)), ((), ()))


def dot(a, b, dims):
    return lax.dot_general(a, b, dims, preferred_element_type=F32)


def kernel(
    ids_ref, scale_ref, x_hbm, dy_hbm, wg_hbm, wu_hbm, wd_hbm,
    in_grad_hbm, gate_hbm, up_hbm, down_hbm,
    tok, wgu, wd, place, ysend, yrecv, back, rows, gu, hid, ggug, act,
    sf, rf, sn, rn, part, rf2, rn2, final, stage, stage_d,
    load_sem, y_send_sem, y_recv_sem, b_send_sem, b_recv_sem,
    ag_send, ag_recv, rs_send, rs_recv, out_sem, out_d_sem,
):
    n_out = ysend.shape[1]
    width = tok.shape[2]
    half = width // 2
    quarter = width // 4
    slots = n_out * CAP
    me_o = lax.axis_index("outer")
    me_i = lax.axis_index("inner")
    my_z = me_i // SIDE
    my_x = lax.rem(me_i, SIDE)

    def ring(v, k):
        return lax.rem(v + k, SIDE)

    def peer(d):
        return lax.rem(me_o + d, n_out)

    first = (my_x, my_z)
    second = (my_z, my_x)

    def block(a, f, s):
        return s * SIDE + f if a == 0 else f * SIDE + s

    barrier = pltpu.get_barrier_semaphore()
    plane = [
        my_z * SIDE + ring(my_x, 1), my_z * SIDE + ring(my_x, 3),
        ring(my_z, 1) * SIDE + my_x, ring(my_z, 3) * SIDE + my_x,
    ]
    for i in plane:
        pl.semaphore_signal(barrier, inc=1, device_id=(me_o, i), device_id_type=MESH)
    for d in range(1, n_out):
        pl.semaphore_signal(barrier, inc=1, device_id=(peer(d), me_i), device_id_type=MESH)

    loads = [
        pltpu.make_async_copy(x_hbm, tok.at[0], load_sem.at[0]),
        pltpu.make_async_copy(dy_hbm, tok.at[1], load_sem.at[1]),
        pltpu.make_async_copy(wg_hbm, wgu.at[:, pl.ds(0, 128)], load_sem.at[2]),
        pltpu.make_async_copy(wu_hbm, wgu.at[:, pl.ds(128, 128)], load_sem.at[3]),
        pltpu.make_async_copy(wd_hbm, wd, load_sem.at[4]),
    ]
    for c in loads:
        c.start()

    toks = ids_ref.shape[0]
    cols = n_out * PAD
    col = lax.broadcasted_iota(jnp.int32, (toks, cols), 1)
    col_expert = col // PAD
    col_slot = lax.rem(col, PAD)
    named = jnp.zeros((toks, cols), F32)
    weight = jnp.zeros((toks, cols), F32)
    for k in range(ids_ref.shape[1]):
        hit = ids_ref[:, k : k + 1] == col_expert
        named = named + jnp.where(hit, 1.0, 0.0)
        weight = weight + jnp.where(hit, scale_ref[:, k : k + 1], 0.0)
    earlier = jnp.where(
        lax.broadcasted_iota(jnp.int32, (toks, toks), 0)
        > lax.broadcasted_iota(jnp.int32, (toks, toks), 1),
        1.0,
        0.0,
    ).astype(BF)
    position = dot(earlier, named.astype(BF), NN)
    chosen = jnp.where(position == col_slot.astype(F32), named, 0.0)
    place[...] = chosen.astype(BF)
    slot_scale = jnp.sum(jnp.transpose(chosen * weight), axis=1, keepdims=True)
    place_t = jnp.transpose(chosen).astype(BF)

    cw = 1024
    n_c = width // cw

    def span(j, w=cw):
        return pl.ds(pl.multiple_of(j * w, w), w)

    def pick(a):
        def step(j, carry):
            v = dot(place_t, tok[a, :, span(j)], NN)
            if a == 1:
                v = v * slot_scale
            ysend[a, :, :, span(j)] = v.astype(BF).reshape(n_out, PAD, cw)
            return carry

        lax.fori_loop(0, n_c, step, 0)
        yrecv[a, me_o] = ysend[a, me_o]

    def y_copy(a, d):
        return pltpu.make_async_remote_copy(
            src_ref=ysend.at[a, peer(d)],
            dst_ref=yrecv.at[a, me_o],
            send_sem=y_send_sem.at[a, d],
            recv_sem=y_recv_sem.at[a, d],
            device_id=(peer(d), me_i),
            device_id_type=MESH,
        )

    y_copies = [[y_copy(a, d) for d in range(1, n_out)] for a in range(2)]
    loads[0].wait()
    pick(0)
    pl.semaphore_wait(barrier, len(plane) + n_out - 1)
    for c in y_copies[0]:
        c.start()
    loads[1].wait()
    pick(1)
    for c in y_copies[1]:
        c.start()

    row = lax.broadcasted_iota(jnp.int32, (slots, cols), 0)
    pcol = lax.broadcasted_iota(jnp.int32, (slots, cols), 1)
    compact = jnp.where((row // CAP) * PAD + lax.rem(row, CAP) == pcol, 1.0, 0.0).astype(BF)

    def gather_own(a):
        for d in range(1, n_out):
            pltpu.make_async_remote_copy(
                src_ref=ysend.at[a, 0],
                dst_ref=yrecv.at[a, lax.rem(me_o + n_out - d, n_out)],
                send_sem=y_send_sem.at[a, d],
                recv_sem=y_recv_sem.at[a, d],
                device_id=(peer(d), me_i),
                device_id_type=MESH,
            ).wait_recv()

        def step(j, carry):
            v = yrecv[a, :, :, span(j)].reshape(cols, cw)
            rows[a, me_i, :, span(j)] = dot(compact, v, NN).astype(BF)
            return carry

        lax.fori_loop(0, n_c, step, 0)

    started = []

    def piece(a, f, s, h):
        ref = rows.at[a, block(a, f, s)]
        return ref if h is None else ref.at[:, pl.ds(h * half, half)]

    def ag(a, k, f, s, h, f_to, s_to):
        c = pltpu.make_async_remote_copy(
            src_ref=piece(a, f, s, h),
            dst_ref=piece(a, f, s, h),
            send_sem=ag_send.at[a, k],
            recv_sem=ag_recv.at[a, k],
            device_id=(me_o, block(a, f_to, s_to)),
            device_id_type=MESH,
        )
        c.start()
        started.append(c)

    def ag_wait(a, k, f, s, h):
        pltpu.make_async_remote_copy(
            src_ref=piece(a, f, s, h),
            dst_ref=piece(a, f, s, h),
            send_sem=ag_send.at[a, k],
            recv_sem=ag_recv.at[a, k],
            device_id=(me_o, block(a, first[a], second[a])),
            device_id_type=MESH,
        ).wait_recv()

    def out_second(a, off):
        f, s = first[a], second[a]
        ag(a, 4 + off, ring(f, off), s, None, f, ring(s, 1))
        ag(a, 8 + off, ring(f, off), s, None, f, ring(s, 3))

    def on_second_plus(a, off):
        f, s = ring(first[a], off), second[a]
        ag_wait(a, 4 + off, f, ring(s, 3), None)
        ag(a, 12 + off, f, ring(s, 3), 0, first[a], ring(s, 1))

    def on_second_minus(a, off):
        f, s = ring(first[a], off), second[a]
        ag_wait(a, 8 + off, f, ring(s, 1), None)
        ag(a, 16 + off, f, ring(s, 1), 1, first[a], ring(s, 3))

    def on_second_far(a, off):
        f, s = ring(first[a], off), second[a]
        ag_wait(a, 12 + off, f, ring(s, 2), 0)
        ag_wait(a, 16 + off, f, ring(s, 2), 1)

    def round0(a):
        f, s = first[a], second[a]
        ag(a, 0, f, s, None, ring(f, 1), s)
        ag(a, 1, f, s, None, ring(f, 3), s)
        out_second(a, 0)

    def round1(a):
        f, s = first[a], second[a]
        ag_wait(a, 0, ring(f, 3), s, None)
        ag(a, 2, ring(f, 3), s, 0, ring(f, 1), s)
        out_second(a, 3)
        ag_wait(a, 1, ring(f, 1), s, None)
        ag(a, 3, ring(f, 1), s, 1, ring(f, 3), s)
        out_second(a, 1)
        on_second_plus(a, 0)
        on_second_minus(a, 0)

    def round2(a):
        f, s = first[a], second[a]
        ag_wait(a, 2, ring(f, 2), s, 0)
        ag_wait(a, 3, ring(f, 2), s, 1)
        out_second(a, 2)
        for off in (3, 1):
            on_second_plus(a, off)
            on_second_minus(a, off)

    def round3(a):
        on_second_plus(a, 2)
        on_second_minus(a, 2)

    def forward(a, blocks):
        for off_f, off_s in blocks:
            b = block(a, ring(first[a], off_f), ring(second[a], off_s))
            if a == 0:

                def step(j, acc, b=b):
                    return acc + dot(rows[0, b, :, span(j)], wgu[span(j), :], NN)

                gu[b] = lax.fori_loop(0, n_c, step, jnp.zeros((slots, 256), F32))
            else:

                def step(j, acc, b=b):
                    return acc + dot(rows[1, b, :, span(j)], wd[:, span(j)], NT)

                hid[b] = lax.fori_loop(0, n_c, step, jnp.zeros((slots, 128), F32))

    gather_own(0)
    round0(0)
    gather_own(1)
    round0(1)
    for c in loads[2:]:
        c.wait()
    for a in range(2):
        forward(a, [(0, 0)])
    round1(0)
    round1(1)
    for a in range(2):
        forward(a, [(1, 0), (3, 0), (0, 1), (0, 3)])
    round2(0)
    round2(1)
    for a in range(2):
        on_second_far(a, 0)
        forward(a, [(2, 0), (1, 1), (3, 1), (1, 3), (3, 3), (0, 2)])
    round3(0)
    round3(1)
    for a in range(2):
        on_second_far(a, 1)
        on_second_far(a, 3)
        forward(a, [(2, 1), (2, 3), (1, 2), (3, 2)])
    for a in range(2):
        on_second_far(a, 2)
        forward(a, [(2, 2)])

    def nonlinear(b, carry):
        gate = gu[b, :, 0:128]
        up = gu[b, :, 128:256]
        grad = hid[b]
        sig = jax.nn.sigmoid(gate)
        silu = gate * sig
        act[b] = (silu * up).astype(BF)
        ggug[b, :, 0:128] = (grad * up * sig * (1.0 + gate * (1.0 - sig))).astype(BF)
        ggug[b, :, 128:256] = (grad * silu).astype(BF)
        return carry

    lax.fori_loop(0, SIDE * SIDE, nonlinear, 0)

    tw = 512
    n_t = half // tw
    p_of = (my_z, my_x)
    q_of = (my_x, my_z)

    def rs_block(a, p, q):
        return p * SIDE + q if a == 0 else q * SIDE + p

    def rs_dev(a, p, q):
        return (me_o, rs_block(a, p, q))

    def rs_copy(a, k, src, dst, p, q):
        return pltpu.make_async_remote_copy(
            src_ref=src,
            dst_ref=dst,
            send_sem=rs_send.at[a, k],
            recv_sem=rs_recv.at[a, k],
            device_id=rs_dev(a, p, q),
            device_id_type=MESH,
        )

    def terms(a, p, qs, put):
        m = jnp.concatenate([ggug[rs_block(a, p, q)] for q in qs], axis=0)

        def step(j, carry):
            w = wgu[pl.ds(pl.multiple_of(a * half + j * tw, tw), tw), :]
            v = dot(m, w, NT).reshape(len(qs), slots, tw)
            put(v, span(j, tw))
            return carry

        lax.fori_loop(0, n_t, step, 0)

    lo, hi = pl.ds(0, 2), pl.ds(2, 2)

    def phase_copies(a):
        p, q = p_of[a], q_of[a]
        up, dn = (ring(p, 1), q), (ring(p, 3), q)
        qu, qd = (p, ring(q, 1)), (p, ring(q, 3))
        c0, c1 = pl.ds(0, quarter), pl.ds(quarter, quarter)
        far, nxt, prv = part.at[a, ring(q, 2)], part.at[a, ring(q, 1)], part.at[a, ring(q, 3)]
        return [
            rs_copy(a, 0, sf.at[a, 0], rf.at[a, 0], *up),
            rs_copy(a, 1, sf.at[a, 1], rf.at[a, 1], *dn),
            rs_copy(a, 2, sn.at[a, 0, hi], rn.at[a, 0, hi], *up),
            rs_copy(a, 3, sn.at[a, 1, lo], rn.at[a, 1, lo], *dn),
            rs_copy(a, 4, sn.at[a, 0, lo], rn.at[a, 0, lo], *up),
            rs_copy(a, 5, sn.at[a, 1, hi], rn.at[a, 1, hi], *dn),
            rs_copy(a, 6, far.at[:, c0], rf2.at[a, 0], *qu),
            rs_copy(a, 7, far.at[:, c1], rf2.at[a, 1], *qd),
            rs_copy(a, 8, nxt.at[:, c1], rn2.at[a, 0, :, c1], *qu),
            rs_copy(a, 9, prv.at[:, c0], rn2.at[a, 1, :, c0], *qd),
            rs_copy(a, 10, nxt.at[:, c0], rn2.at[a, 0, :, c0], *qu),
            rs_copy(a, 11, prv.at[:, c1], rn2.at[a, 1, :, c1], *qd),
        ]

    rs = [phase_copies(a) for a in range(2)]

    for a in range(2):

        def put_far(v, s, a=a):
            sf[a, 0, :, :, s] = v[0:2].astype(BF)
            sf[a, 1, :, :, s] = v[2:4].astype(BF)

        terms(a, ring(p_of[a], 2), (0, 1, 2, 3), put_far)
        rs[a][0].start()
        rs[a][1].start()
    for a in range(2):

        def put_up(v, s, a=a):
            sn[a, 0, 2:4, :, s] = v.astype(BF)

        def put_dn(v, s, a=a):
            sn[a, 1, 0:2, :, s] = v.astype(BF)

        terms(a, ring(p_of[a], 1), (2, 3), put_up)
        rs[a][2].start()
        terms(a, ring(p_of[a], 3), (0, 1), put_dn)
        rs[a][3].start()

    gw = 512

    def grad_step(j, carry):
        slot = lax.rem(j, 2)

        def outs(i):
            dst = pl.ds(pl.multiple_of(i * gw, gw), gw)
            return (
                pltpu.make_async_copy(
                    stage.at[slot, :, pl.ds(0, 128)], gate_hbm.at[dst, :], out_sem.at[0, slot]
                ),
                pltpu.make_async_copy(
                    stage.at[slot, :, pl.ds(128, 128)], up_hbm.at[dst, :], out_sem.at[1, slot]
                ),
            )

        @pl.when(j >= 2)
        def _():
            for c in outs(j - 2):
                c.wait()

        xs = rows[0, :, :, span(j, gw)].reshape(SIDE * SIDE * slots, gw)
        stage[slot] = dot(xs, ggug[...].reshape(SIDE * SIDE * slots, 256), TN)
        for c in outs(j):
            c.start()
        return carry

    def down_step(j, carry):
        slot = lax.rem(j, 2)

        def out(i):
            return pltpu.make_async_copy(
                stage_d.at[slot], down_hbm.at[:, span(i, gw)], out_d_sem.at[slot]
            )

        @pl.when(j >= 2)
        def _():
            out(j - 2).wait()

        gs = rows[1, :, :, span(j, gw)].reshape(SIDE * SIDE * slots, gw)
        stage_d[slot] = dot(act[...].reshape(SIDE * SIDE * slots, 128), gs, TN)
        out(j).start()
        return carry

    n_g = width // gw
    lax.fori_loop(0, n_g, down_step, 0)

    for a in range(2):

        def put_up2(v, s, a=a):
            sn[a, 0, 0:2, :, s] = (v + rf[a, 0, :, :, s].astype(F32)).astype(BF)

        def put_dn2(v, s, a=a):
            sn[a, 1, 2:4, :, s] = (v + rf[a, 1, :, :, s].astype(F32)).astype(BF)

        rs[a][0].wait_recv()
        terms(a, ring(p_of[a], 1), (0, 1), put_up2)
        rs[a][4].start()
        rs[a][1].wait_recv()
        terms(a, ring(p_of[a], 3), (2, 3), put_dn2)
        rs[a][5].start()

    lax.fori_loop(0, n_g, grad_step, 0)

    for a in range(2):
        for k in (2, 3, 4, 5):
            rs[a][k].wait_recv()

        def put_part(v, s, a=a):
            t = v + rn[a, 0, :, :, s].astype(F32) + rn[a, 1, :, :, s].astype(F32)
            part[a, :, :, s] = t.astype(BF)

        terms(a, p_of[a], (0, 1, 2, 3), put_part)
        for k in (6, 7, 8, 9):
            rs[a][k].start()
    for a in range(2):
        q = q_of[a]
        c0, c1 = pl.ds(0, quarter), pl.ds(quarter, quarter)
        for k, off, c, r in ((6, 1, c0, 0), (7, 3, c1, 1)):
            rs[a][k].wait_recv()
            b = ring(q, off)
            t = part[a, b, :, c].astype(F32) + rf2[a, r].astype(F32)
            part[a, b, :, c] = t.astype(BF)
            rs[a][k + 4].start()
    for a in range(2):
        for k in (8, 9, 10, 11):
            rs[a][k].wait_recv()
        t = part[a, q_of[a]].astype(F32) + rn2[a, 0].astype(F32) + rn2[a, 1].astype(F32)
        final[:, pl.ds(a * half, half)] = t.astype(BF)

    for c in y_copies[0]:
        c.wait_send()
    spread = jnp.where(
        (lax.broadcasted_iota(jnp.int32, (cols, slots), 1) // CAP) * PAD
        + lax.rem(lax.broadcasted_iota(jnp.int32, (cols, slots), 1), CAP)
        == lax.broadcasted_iota(jnp.int32, (cols, slots), 0),
        1.0,
        0.0,
    ).astype(BF)

    def spread_step(j, carry):
        v = dot(spread, final[:, span(j)], NN).astype(BF)
        ysend[0, :, :, span(j)] = v.reshape(n_out, PAD, cw)
        return carry

    lax.fori_loop(0, n_c, spread_step, 0)
    back_copies = []
    for d in range(1, n_out):
        c = pltpu.make_async_remote_copy(
            src_ref=ysend.at[0, peer(d)],
            dst_ref=back.at[me_o],
            send_sem=b_send_sem.at[d],
            recv_sem=b_recv_sem.at[d],
            device_id=(peer(d), me_i),
            device_id_type=MESH,
        )
        c.start()
        back_copies.append(c)
    back[me_o] = ysend[0, me_o]
    for d in range(1, n_out):
        pltpu.make_async_remote_copy(
            src_ref=ysend.at[0, 0],
            dst_ref=back.at[lax.rem(me_o + n_out - d, n_out)],
            send_sem=b_send_sem.at[d],
            recv_sem=b_recv_sem.at[d],
            device_id=(peer(d), me_i),
            device_id_type=MESH,
        ).wait_recv()

    def in_step(j, carry):
        v = back[:, :, span(j)].reshape(cols, cw)
        tok[0, :, span(j)] = dot(place[...], v, NN).astype(BF)
        return carry

    lax.fori_loop(0, n_c, in_step, 0)
    in_out = pltpu.make_async_copy(tok.at[0], in_grad_hbm, load_sem.at[0])
    in_out.start()

    for c in started:
        c.wait_send()
    for c in y_copies[1]:
        c.wait_send()
    for c in back_copies:
        c.wait_send()
    for a in range(2):
        for c in rs[a]:
            c.wait_send()
    for i in (n_g - 2, n_g - 1):
        slot = i % 2
        dst = pl.ds(i * gw, gw)
        pltpu.make_async_copy(
            stage.at[slot, :, pl.ds(0, 128)], gate_hbm.at[dst, :], out_sem.at[0, slot]
        ).wait()
        pltpu.make_async_copy(
            stage.at[slot, :, pl.ds(128, 128)], up_hbm.at[dst, :], out_sem.at[1, slot]
        ).wait()
        pltpu.make_async_copy(
            stage_d.at[slot], down_hbm.at[:, dst], out_d_sem.at[slot]
        ).wait()
    in_out.wait()


def shards(layer_input, out_grad, expert_ids, route_scales, w_gate, w_up, w_down):
    toks, width = layer_input.shape
    n_out = lax.axis_size("outer")
    n_in = lax.axis_size("inner")
    hidden = w_gate.shape[2]
    slots = n_out * CAP
    half, quarter = width // 2, width // 4
    any_spec = pl.BlockSpec(memory_space=pl.ANY)
    vmem = pl.BlockSpec(memory_space=pltpu.VMEM)
    dma = pltpu.SemaphoreType.DMA
    in_grad, gate, up, down = pl.pallas_call(
        kernel,
        out_shape=(
            jax.ShapeDtypeStruct((toks, width), BF),
            jax.ShapeDtypeStruct((width, hidden), F32),
            jax.ShapeDtypeStruct((width, hidden), F32),
            jax.ShapeDtypeStruct((hidden, width), F32),
        ),
        in_specs=[vmem, vmem] + [any_spec] * 5,
        out_specs=(any_spec,) * 4,
        scratch_shapes=[
            pltpu.VMEM((2, toks, width), BF),
            pltpu.VMEM((width, 2 * hidden), BF),
            pltpu.VMEM((hidden, width), BF),
            pltpu.VMEM((toks, n_out * PAD), BF),
            pltpu.VMEM((2, n_out, PAD, width), BF),
            pltpu.VMEM((2, n_out, PAD, width), BF),
            pltpu.VMEM((n_out, PAD, width), BF),
            pltpu.VMEM((2, n_in, slots, width), BF),
            pltpu.VMEM((n_in, slots, 2 * hidden), F32),
            pltpu.VMEM((n_in, slots, hidden), F32),
            pltpu.VMEM((n_in, slots, 2 * hidden), BF),
            pltpu.VMEM((n_in, slots, hidden), BF),
            pltpu.VMEM((2, 2, 2, slots, half), BF),
            pltpu.VMEM((2, 2, 2, slots, half), BF),
            pltpu.VMEM((2, 2, SIDE, slots, half), BF),
            pltpu.VMEM((2, 2, SIDE, slots, half), BF),
            pltpu.VMEM((2, SIDE, slots, half), BF),
            pltpu.VMEM((2, 2, slots, quarter), BF),
            pltpu.VMEM((2, 2, slots, half), BF),
            pltpu.VMEM((slots, width), BF),
            pltpu.VMEM((2, 512, 2 * hidden), F32),
            pltpu.VMEM((2, hidden, 512), F32),
            dma((5,)),
            dma((2, n_out)),
            dma((2, n_out)),
            dma((n_out,)),
            dma((n_out,)),
            dma((2, 20)),
            dma((2, 20)),
            dma((2, 12)),
            dma((2, 12)),
            dma((2, 2)),
            dma((2,)),
        ],
        compiler_params=pltpu.CompilerParams(
            collective_id=0, has_side_effects=True, vmem_limit_bytes=67043328
        ),
        name="expert_backward",
    )(expert_ids, route_scales, layer_input, out_grad, w_gate[0], w_up[0], w_down[0])
    return in_grad, gate[None], up[None], down[None]


def solution(mesh):
    return jax.shard_map(
        shards,
        mesh=mesh,
        in_specs=(
            P(("outer", "inner"), None),
            P(("outer", "inner"), None),
            P(("outer", "inner"), None),
            P(("outer", "inner"), None),
            P("outer", None, "inner"),
            P("outer", None, "inner"),
            P("outer", "inner", None),
        ),
        out_specs=(
            P(("outer", "inner"), None),
            P("outer", None, "inner"),
            P("outer", None, "inner"),
            P("outer", "inner", None),
        ),
        check_vma=False,
    )
```

time: 356 us -> 235 us (0.66)
  Pallas kernels: 0 us -> 219 us
  waiting for transfers between devices: 213 us -> 0 us
  matrix products: 71.7 us -> 0 us
  blocking collectives: 37.4 us -> 0 us
  between operations: 13.9 us -> 0.65 us
  starting transfers between devices: 5.58 us -> 0 us
  local copies, waits for them, and re-layouts: 9.88 us -> 14.4 us
    pallas_call x0 -> x1, Pallas kernels: none -> 219 us  [shards(): pl.pallas_call(kernel, out_shape=(jax.ShapeDtypeStruct((toks, width), BF)...]
    all_gather x2 -> x0, waiting for transfers between devices: 135 us -> none  [the longest x1 74.4 us: shards(): lax.all_gather(got_gy.reshape(-1, model_width), 'inner', axis=0, tiled=True)]
    reduce_scatter x1 -> x0, waiting for transfers between devices: 72.1 us -> none  [shards(): lax.psum_scatter((term + lax.dot_general(up_store, up_w, (((1,), (1,)), (...]
    dot_general x11 -> x0, matrix products: 71.7 us -> none  [the longest x1 13.2 us: shards(): lax.dot_general(up_store, up_w, (((1,), (1,)), ((), ())), preferred_eleme...]
    all_to_all x2 -> x0, blocking collectives: 37.4 us -> none  [the longest x1 19.7 us: shards(): lax.all_to_all(send_x, 'outer', split_axis=0, concat_axis=0, tiled=True)]
    unnamed x12, local copies, waits for them, and re-layouts: 1.63 us -> 14.4 us
    reshape x6 -> x0, local copies, waits for them, and re-layouts: 7.57 us -> none  [the longest x1 2.27 us: shards(): got_x.reshape(-1, model_width)]
    all_to_all x1 -> x0, waiting for transfers between devices: 5.87 us -> none  [shards(): lax.all_to_all(mine, 'outer', split_axis=0, concat_axis=0, tiled=True)]
  transfers between devices with their start and end apart: 4 -> 0, of which waited for: 4 -> 0; matrix products, arithmetic and copies ran while one was open for 12% -> 0% of each run, Pallas kernels for 0% -> 0%
where the time goes in v1:
time: 235 us; the launch traced here: 234 us
  Pallas kernels  219 us (93%)
  local copies, waits for them, and re-layouts  14.4 us (6%)
    pallas_call x1, Pallas kernels, shards(): pl.pallas_call(kernel, out_shape=(jax.ShapeDtypeStruct((toks, width), BF)...  219 us
    unnamed x12, local copies, waits for them, and re-layouts  14.4 us

profile of v1, /device:TPU:1, one launch (start us, length us, event | category | flops | bytes accessed | tf_op | source)
XLA Modules:
  0.0 234.4 jit_solution(5269648217509233412)
XLA Ops:
  0.6 1.4 copy.11.ids_ref
  2.0 1.4 copy.12.scale_ref
  3.5 219.4 %expert_backward.1 = (bf16[128,7168]{1,0:T(8,128)(2,1)}, f32[7168,128]{1,0:T(8,128)}, f32[7168,128]{1,0:T(8,128)}, f32[128,7168]{1,0:T(8,128)}) custom-call(s32[128,8]{1,0:T(8,128)} %copy.11.ids_ref, f32[128,8]{1,0:T(8,128)} %copy.12.scale_ref, bf16[128,7168]{1,0:T(8,128)(2,1)} %x_hbm.1, bf16[128,7168]{1,0:T(8,128)(2,1)} %dy_hbm.1, ...), custom_call_target="tpu_custom_call" | custom-call | tf_op jit(solution)/shard_map/expert_backward/pallas_call | solution.py:541
  222.8 0.0 copy-start.2
  222.8 3.0 %copy.17 = bf16[128,7168]{1,0:T(8,128)(2,1)} copy(bf16[128,7168]{1,0:T(8,128)(2,1)} %get-tuple-element.16) | data formatting | bytes 3670016
  225.8 0.0 copy-done.2
  225.8 0.0 copy-start.1
  225.8 1.9 copy.18
  227.7 1.5 copy-done.1
  229.2 0.0 copy-start
  229.2 1.9 copy.19
  231.1 1.5 copy-done
  232.6 1.8 copy.20
Async XLA Ops:
  222.8 3.0 %copy-start.2 = (f32[7168,128]{1,0:T(8,128)S(1)}, f32[7168,128]{1,0:T(8,128)}, u32[]{:S(2)}) copy-start(f32[7168,128]{1,0:T(8,128)} %get-tuple-element.9) | copy-start | bytes 11010052
  225.8 3.4 %copy-start.1 = (f32[7168,128]{1,0:T(8,128)S(1)}, f32[7168,128]{1,0:T(8,128)}, u32[]{:S(2)}) copy-start(f32[7168,128]{1,0:T(8,128)} %get-tuple-element.10) | copy-start | bytes 11010052
  229.2 3.4 %copy-start = (f32[128,7168]{1,0:T(8,128)S(1)}, f32[128,7168]{1,0:T(8,128)}, u32[]{:S(2)}) copy-start(f32[128,7168]{1,0:T(8,128)} %get-tuple-element.11) | copy-start | bytes 11010052

commit v2 on v1

v2 whole, which is shorter than its diff:
```python
import jax
import jax.numpy as jnp
from jax import lax
from jax.experimental import pallas as pl
from jax.experimental.pallas import tpu as pltpu
from jax.sharding import PartitionSpec as P

CAP = 6
PAD = 8
SIDE = 4
BF = jnp.bfloat16
F32 = jnp.float32
MESH = pl.DeviceIdType.MESH
NN = (((1,), (0,)), ((), ()))
NT = (((1,), (1,)), ((), ()))
TN = (((0,), (0,)), ((), ()))


def dot(a, b, dims):
    return lax.dot_general(a, b, dims, preferred_element_type=F32)


def kernel(
    ids_ref, scale_ref, x_hbm, dy_hbm, wg_hbm, wu_hbm, wd_hbm,
    back_hbm, place_hbm, gate_hbm, up_hbm, down_hbm,
    tok, wgu, wd, place, ysend, yrecv, back, rows, gu, hid, ggug, act,
    sf, rf, sn, rn, part, rf2, rn2, stage, stage_d,
    load_sem, y_send_sem, y_recv_sem, b_send_sem, b_recv_sem,
    ag_send, ag_recv, rs_send, rs_recv, out_sem, out_d_sem, b_out_sem, place_sem,
):
    n_out = ysend.shape[1]
    width = tok.shape[2]
    half = width // 2
    quarter = width // 4
    eighth = width // 8
    slots = n_out * CAP
    me_o = lax.axis_index("outer")
    me_i = lax.axis_index("inner")
    my_z = me_i // SIDE
    my_x = lax.rem(me_i, SIDE)

    def ring(v, k):
        return lax.rem(v + k, SIDE)

    def peer(d):
        return lax.rem(me_o + d, n_out)

    first = (my_x, my_z)
    second = (my_z, my_x)

    def block(a, f, s):
        return s * SIDE + f if a == 0 else f * SIDE + s

    barrier = pltpu.get_barrier_semaphore()
    plane = [
        my_z * SIDE + ring(my_x, 1), my_z * SIDE + ring(my_x, 3),
        ring(my_z, 1) * SIDE + my_x, ring(my_z, 3) * SIDE + my_x,
    ]
    for i in plane:
        pl.semaphore_signal(barrier, inc=1, device_id=(me_o, i), device_id_type=MESH)
    for d in range(1, n_out):
        pl.semaphore_signal(barrier, inc=1, device_id=(peer(d), me_i), device_id_type=MESH)

    loads = [
        pltpu.make_async_copy(x_hbm, tok.at[0], load_sem.at[0]),
        pltpu.make_async_copy(dy_hbm, tok.at[1], load_sem.at[1]),
        pltpu.make_async_copy(wg_hbm, wgu.at[:, pl.ds(0, 128)], load_sem.at[2]),
        pltpu.make_async_copy(wu_hbm, wgu.at[:, pl.ds(128, 128)], load_sem.at[3]),
        pltpu.make_async_copy(wd_hbm, wd, load_sem.at[4]),
    ]
    for c in loads:
        c.start()

    ids = jnp.transpose(ids_ref[...].astype(F32))
    scales = jnp.transpose(scale_ref[...])
    toks = ids.shape[0]
    cols = n_out * PAD
    col = lax.broadcasted_iota(jnp.int32, (toks, cols), 1)
    col_expert = (col // PAD).astype(F32)
    col_slot = lax.rem(col, PAD)
    named = jnp.zeros((toks, cols), F32)
    weight = jnp.zeros((toks, cols), F32)
    for k in range(ids.shape[1]):
        hit = ids[:, k : k + 1] == col_expert
        named = named + jnp.where(hit, 1.0, 0.0)
        weight = weight + jnp.where(hit, scales[:, k : k + 1], 0.0)
    earlier = jnp.where(
        lax.broadcasted_iota(jnp.int32, (toks, toks), 0)
        > lax.broadcasted_iota(jnp.int32, (toks, toks), 1),
        1.0,
        0.0,
    ).astype(BF)
    position = dot(earlier, named.astype(BF), NN)
    chosen = jnp.where(position == col_slot.astype(F32), named, 0.0)
    place[...] = chosen.astype(BF)
    place_out = pltpu.make_async_copy(place, place_hbm, place_sem)
    place_out.start()
    slot_scale = jnp.sum(jnp.transpose(chosen * weight), axis=1, keepdims=True)
    place_t = jnp.transpose(chosen).astype(BF)

    cw = 1024
    n_c = width // cw

    def span(j, w=cw):
        return pl.ds(pl.multiple_of(j * w, w), w)

    def part_span(first_col, j):
        return pl.ds(pl.multiple_of(first_col + j * eighth, eighth), eighth)

    def pick(a, h):
        def step(j, carry):
            s = part_span(h * half, j)
            v = dot(place_t, tok[a, :, s], NN)
            if a == 1:
                v = v * slot_scale
            ysend[a, :, :, s] = v.astype(BF).reshape(n_out, PAD, eighth)
            return carry

        lax.fori_loop(0, 4, step, 0)
        own = pl.ds(h * half, half)
        yrecv[a, me_o, :, own] = ysend[a, me_o, :, own]

    def y_copy(a, h, d):
        own = pl.ds(h * half, half)
        return pltpu.make_async_remote_copy(
            src_ref=ysend.at[a, peer(d), :, own],
            dst_ref=yrecv.at[a, me_o, :, own],
            send_sem=y_send_sem.at[a, h, d],
            recv_sem=y_recv_sem.at[a, h, d],
            device_id=(peer(d), me_i),
            device_id_type=MESH,
        )

    y_copies = [[], []]
    for a in range(2):
        loads[a].wait()
        for h in range(2):
            pick(a, h)
            if a == 0 and h == 0:
                pl.semaphore_wait(barrier, len(plane) + n_out - 1)
            for d in range(1, n_out):
                c = y_copy(a, h, d)
                c.start()
                y_copies[a].append(c)

    row = lax.broadcasted_iota(jnp.int32, (slots, cols), 0)
    pcol = lax.broadcasted_iota(jnp.int32, (slots, cols), 1)
    compact = jnp.where((row // CAP) * PAD + lax.rem(row, CAP) == pcol, 1.0, 0.0).astype(BF)

    def gather_own(a, h):
        own = pl.ds(h * half, half)
        for d in range(1, n_out):
            pltpu.make_async_remote_copy(
                src_ref=ysend.at[a, 0, :, own],
                dst_ref=yrecv.at[a, lax.rem(me_o + n_out - d, n_out), :, own],
                send_sem=y_send_sem.at[a, h, d],
                recv_sem=y_recv_sem.at[a, h, d],
                device_id=(peer(d), me_i),
                device_id_type=MESH,
            ).wait_recv()

        def step(j, carry):
            s = part_span(h * half, j)
            v = yrecv[a, :, :, s].reshape(cols, eighth)
            rows[a, me_i, :, s] = dot(compact, v, NN).astype(BF)
            return carry

        lax.fori_loop(0, 4, step, 0)

    started = []

    def piece(a, f, s, h):
        ref = rows.at[a, block(a, f, s)]
        return ref if h is None else ref.at[:, pl.ds(h * half, half)]

    def ag(a, k, f, s, h, f_to, s_to):
        c = pltpu.make_async_remote_copy(
            src_ref=piece(a, f, s, h),
            dst_ref=piece(a, f, s, h),
            send_sem=ag_send.at[a, k, h or 0],
            recv_sem=ag_recv.at[a, k, h or 0],
            device_id=(me_o, block(a, f_to, s_to)),
            device_id_type=MESH,
        )
        c.start()
        started.append(c)

    def ag_wait(a, k, f, s, h):
        pltpu.make_async_remote_copy(
            src_ref=piece(a, f, s, h),
            dst_ref=piece(a, f, s, h),
            send_sem=ag_send.at[a, k, h or 0],
            recv_sem=ag_recv.at[a, k, h or 0],
            device_id=(me_o, block(a, first[a], second[a])),
            device_id_type=MESH,
        ).wait_recv()

    def out_second(a, off):
        f, s = first[a], second[a]
        ag(a, 4 + off, ring(f, off), s, None, f, ring(s, 1))
        ag(a, 8 + off, ring(f, off), s, None, f, ring(s, 3))

    def on_second_plus(a, off):
        f, s = ring(first[a], off), second[a]
        for h in (0, 1) if off == 0 else (None,):
            ag_wait(a, 4 + off, f, ring(s, 3), h)
        ag(a, 12 + off, f, ring(s, 3), 0, first[a], ring(s, 1))

    def on_second_minus(a, off):
        f, s = ring(first[a], off), second[a]
        for h in (0, 1) if off == 0 else (None,):
            ag_wait(a, 8 + off, f, ring(s, 1), h)
        ag(a, 16 + off, f, ring(s, 1), 1, first[a], ring(s, 3))

    def on_second_far(a, off):
        f, s = ring(first[a], off), second[a]
        ag_wait(a, 12 + off, f, ring(s, 2), 0)
        ag_wait(a, 16 + off, f, ring(s, 2), 1)

    def round0(a, h):
        f, s = first[a], second[a]
        ag(a, 0, f, s, h, ring(f, 1), s)
        ag(a, 1, f, s, h, ring(f, 3), s)
        ag(a, 4, f, s, h, f, ring(s, 1))
        ag(a, 8, f, s, h, f, ring(s, 3))

    def round1(a):
        f, s = first[a], second[a]
        ag_wait(a, 0, ring(f, 3), s, 0)
        ag(a, 2, ring(f, 3), s, 0, ring(f, 1), s)
        ag_wait(a, 0, ring(f, 3), s, 1)
        out_second(a, 3)
        ag_wait(a, 1, ring(f, 1), s, 0)
        ag_wait(a, 1, ring(f, 1), s, 1)
        ag(a, 3, ring(f, 1), s, 1, ring(f, 3), s)
        out_second(a, 1)
        on_second_plus(a, 0)
        on_second_minus(a, 0)

    def round2(a):
        f, s = first[a], second[a]
        ag_wait(a, 2, ring(f, 2), s, 0)
        ag_wait(a, 3, ring(f, 2), s, 1)
        out_second(a, 2)
        for off in (3, 1):
            on_second_plus(a, off)
            on_second_minus(a, off)

    def round3(a):
        on_second_plus(a, 2)
        on_second_minus(a, 2)

    def forward(a, blocks):
        for off_f, off_s in blocks:
            b = block(a, ring(first[a], off_f), ring(second[a], off_s))
            if a == 0:

                def step(j, acc, b=b):
                    return acc + dot(rows[0, b, :, span(j)], wgu[span(j), :], NN)

                gu[b] = lax.fori_loop(0, n_c, step, jnp.zeros((slots, 256), F32))
            else:

                def step(j, acc, b=b):
                    return acc + dot(rows[1, b, :, span(j)], wd[:, span(j)], NT)

                hid[b] = lax.fori_loop(0, n_c, step, jnp.zeros((slots, 128), F32))

    for a in range(2):
        for h in range(2):
            gather_own(a, h)
            round0(a, h)
    for c in loads[2:]:
        c.wait()
    for a in range(2):
        forward(a, [(0, 0)])
    round1(0)
    round1(1)
    for a in range(2):
        forward(a, [(1, 0), (3, 0), (0, 1), (0, 3)])
    round2(0)
    round2(1)
    for a in range(2):
        on_second_far(a, 0)
        forward(a, [(2, 0), (1, 1), (3, 1), (1, 3), (3, 3), (0, 2)])
    round3(0)
    round3(1)
    for a in range(2):
        on_second_far(a, 1)
        on_second_far(a, 3)
        forward(a, [(2, 1), (2, 3), (1, 2), (3, 2)])
    def nonlinear(b, carry):
        gate = gu[b, :, 0:128]
        up = gu[b, :, 128:256]
        grad = hid[b]
        sig = jax.nn.sigmoid(gate)
        silu = gate * sig
        act[b] = (silu * up).astype(BF)
        ggug[b, :, 0:128] = (grad * up * sig * (1.0 + gate * (1.0 - sig))).astype(BF)
        ggug[b, :, 128:256] = (grad * silu).astype(BF)
        return carry

    last = ring(my_z, 2) * SIDE + ring(my_x, 2)

    def nonlinear_early(j, carry):
        return nonlinear(lax.rem(last + j, SIDE * SIDE), carry)

    lax.fori_loop(1, SIDE * SIDE, nonlinear_early, 0)

    p_of = (my_z, my_x)
    q_of = (my_x, my_z)

    def rs_block(a, p, q):
        return p * SIDE + q if a == 0 else q * SIDE + p

    def rs_dev(a, p, q):
        return (me_o, rs_block(a, p, q))

    def rs_copy(a, c, k, src, dst, p, q):
        return pltpu.make_async_remote_copy(
            src_ref=src,
            dst_ref=dst,
            send_sem=rs_send.at[a, c, k],
            recv_sem=rs_recv.at[a, c, k],
            device_id=rs_dev(a, p, q),
            device_id_type=MESH,
        )

    def terms(a, c, p, qs, put):
        m = jnp.concatenate([ggug[rs_block(a, p, q)] for q in qs], axis=0)

        def step(j, carry):
            w = wgu[part_span(a * half + c * quarter, j), :]
            v = dot(m, w, NT).reshape(len(qs), slots, eighth)
            put(v, part_span(c * quarter, j))
            return carry

        lax.fori_loop(0, 2, step, 0)

    lo, hi = pl.ds(0, 2), pl.ds(2, 2)

    def phase_copies(a, c):
        p, q = p_of[a], q_of[a]
        up, dn = (ring(p, 1), q), (ring(p, 3), q)
        qu, qd = (p, ring(q, 1)), (p, ring(q, 3))
        cc = pl.ds(c * quarter, quarter)
        c0, c1 = pl.ds(c * quarter, eighth), pl.ds(c * quarter + eighth, eighth)
        ce = pl.ds(c * eighth, eighth)
        far, nxt, prv = part.at[a, ring(q, 2)], part.at[a, ring(q, 1)], part.at[a, ring(q, 3)]
        return [
            rs_copy(a, c, 0, sf.at[a, 0, :, :, cc], rf.at[a, 0, :, :, cc], *up),
            rs_copy(a, c, 1, sf.at[a, 1, :, :, cc], rf.at[a, 1, :, :, cc], *dn),
            rs_copy(a, c, 2, sn.at[a, 0, hi, :, cc], rn.at[a, 0, hi, :, cc], *up),
            rs_copy(a, c, 3, sn.at[a, 1, lo, :, cc], rn.at[a, 1, lo, :, cc], *dn),
            rs_copy(a, c, 4, sn.at[a, 0, lo, :, cc], rn.at[a, 0, lo, :, cc], *up),
            rs_copy(a, c, 5, sn.at[a, 1, hi, :, cc], rn.at[a, 1, hi, :, cc], *dn),
            rs_copy(a, c, 6, far.at[:, c0], rf2.at[a, 0, :, ce], *qu),
            rs_copy(a, c, 7, far.at[:, c1], rf2.at[a, 1, :, ce], *qd),
            rs_copy(a, c, 8, nxt.at[:, c1], rn2.at[a, 0, :, c1], *qu),
            rs_copy(a, c, 9, prv.at[:, c0], rn2.at[a, 1, :, c0], *qd),
            rs_copy(a, c, 10, nxt.at[:, c0], rn2.at[a, 0, :, c0], *qu),
            rs_copy(a, c, 11, prv.at[:, c1], rn2.at[a, 1, :, c1], *qd),
        ]

    rs = [[phase_copies(a, c) for c in range(2)] for a in range(2)]

    def near_at_once(a, c):
        def put_up(v, s):
            sn[a, 0, 2:4, :, s] = v.astype(BF)

        def put_dn(v, s):
            sn[a, 1, 0:2, :, s] = v.astype(BF)

        terms(a, c, ring(p_of[a], 1), (2, 3), put_up)
        rs[a][c][2].start()
        terms(a, c, ring(p_of[a], 3), (0, 1), put_dn)
        rs[a][c][3].start()

    def far_part(a, c):
        def put_far(v, s):
            sf[a, 0, :, :, s] = v[0:2].astype(BF)
            sf[a, 1, :, :, s] = v[2:4].astype(BF)

        terms(a, c, ring(p_of[a], 2), (0, 1, 2, 3), put_far)
        rs[a][c][0].start()
        rs[a][c][1].start()

    def near_after(a, c):
        def put_up2(v, s):
            sn[a, 0, 0:2, :, s] = (v + rf[a, 0, :, :, s].astype(F32)).astype(BF)

        def put_dn2(v, s):
            sn[a, 1, 2:4, :, s] = (v + rf[a, 1, :, :, s].astype(F32)).astype(BF)

        rs[a][c][0].wait_recv()
        terms(a, c, ring(p_of[a], 1), (0, 1), put_up2)
        rs[a][c][4].start()
        rs[a][c][1].wait_recv()
        terms(a, c, ring(p_of[a], 3), (2, 3), put_dn2)
        rs[a][c][5].start()

    for a in range(2):
        near_at_once(a, 0)
    for a in range(2):
        on_second_far(a, 2)
        forward(a, [(2, 2)])
    nonlinear(last, 0)
    for c in range(2):
        for a in range(2):
            far_part(a, c)
    for a in range(2):
        near_at_once(a, 1)

    gw = 512

    def grad_step(j, carry):
        slot = lax.rem(j, 2)

        def outs(i):
            dst = pl.ds(pl.multiple_of(i * gw, gw), gw)
            return (
                pltpu.make_async_copy(
                    stage.at[slot, :, pl.ds(0, 128)], gate_hbm.at[dst, :], out_sem.at[0, slot]
                ),
                pltpu.make_async_copy(
                    stage.at[slot, :, pl.ds(128, 128)], up_hbm.at[dst, :], out_sem.at[1, slot]
                ),
            )

        @pl.when(j >= 2)
        def _():
            for c in outs(j - 2):
                c.wait()

        xs = rows[0, :, :, span(j, gw)].reshape(SIDE * SIDE * slots, gw)
        stage[slot] = dot(xs, ggug[...].reshape(SIDE * SIDE * slots, 256), TN)
        for c in outs(j):
            c.start()
        return carry

    def down_step(j, carry):
        slot = lax.rem(j, 2)

        def out(i):
            return pltpu.make_async_copy(
                stage_d.at[slot], down_hbm.at[:, span(i, gw)], out_d_sem.at[slot]
            )

        @pl.when(j >= 2)
        def _():
            out(j - 2).wait()

        gs = rows[1, :, :, span(j, gw)].reshape(SIDE * SIDE * slots, gw)
        stage_d[slot] = dot(act[...].reshape(SIDE * SIDE * slots, 128), gs, TN)
        out(j).start()
        return carry

    n_g = width // gw
    lax.fori_loop(0, n_g, down_step, 0)
    for c in range(2):
        for a in range(2):
            near_after(a, c)
    lax.fori_loop(0, n_g, grad_step, 0)

    for c in range(2):
        for a in range(2):
            for k in (2, 3, 4, 5):
                rs[a][c][k].wait_recv()

            def put_part(v, s, a=a):
                t = v + rn[a, 0, :, :, s].astype(F32) + rn[a, 1, :, :, s].astype(F32)
                part[a, :, :, s] = t.astype(BF)

            terms(a, c, p_of[a], (0, 1, 2, 3), put_part)
            for k in (6, 7, 8, 9):
                rs[a][c][k].start()
    for c in range(2):
        ce = pl.ds(c * eighth, eighth)
        for a in range(2):
            for k, off, col0, r in ((6, 1, 0, 0), (7, 3, eighth, 1)):
                rs[a][c][k].wait_recv()
                b = ring(q_of[a], off)
                s = pl.ds(c * quarter + col0, eighth)
                t = part[a, b, :, s].astype(F32) + rf2[a, r, :, ce].astype(F32)
                part[a, b, :, s] = t.astype(BF)
                rs[a][c][k + 4].start()

    for c in y_copies[0]:
        c.wait_send()
    spread = jnp.where(
        (lax.broadcasted_iota(jnp.int32, (cols, slots), 1) // CAP) * PAD
        + lax.rem(lax.broadcasted_iota(jnp.int32, (cols, slots), 1), CAP)
        == lax.broadcasted_iota(jnp.int32, (cols, slots), 0),
        1.0,
        0.0,
    ).astype(BF)
    back_copies = []
    for c in range(2):
        for a in range(2):
            for k in (8, 9, 10, 11):
                rs[a][c][k].wait_recv()
            first_col = a * half + c * quarter

            def final_step(j, carry, a=a, c=c, first_col=first_col):
                s = part_span(c * quarter, j)
                t = part[a, q_of[a], :, s].astype(F32) + rn2[a, 0, :, s].astype(F32)
                t = (t + rn2[a, 1, :, s].astype(F32)).astype(BF)
                v = dot(spread, t, NN).astype(BF).reshape(n_out, PAD, eighth)
                ysend[0, :, :, part_span(first_col, j)] = v
                return carry

            lax.fori_loop(0, 2, final_step, 0)
            seg = pl.ds(first_col, quarter)
            for d in range(1, n_out):
                copy = pltpu.make_async_remote_copy(
                    src_ref=ysend.at[0, peer(d), :, seg],
                    dst_ref=back.at[me_o, :, seg],
                    send_sem=b_send_sem.at[a, c, d],
                    recv_sem=b_recv_sem.at[a, c, d],
                    device_id=(peer(d), me_i),
                    device_id_type=MESH,
                )
                copy.start()
                back_copies.append(copy)
            back[me_o, :, seg] = ysend[0, me_o, :, seg]
    back_outs = []
    for c in range(2):
        for a in range(2):
            seg = pl.ds(a * half + c * quarter, quarter)
            for d in range(1, n_out):
                pltpu.make_async_remote_copy(
                    src_ref=ysend.at[0, 0, :, seg],
                    dst_ref=back.at[lax.rem(me_o + n_out - d, n_out), :, seg],
                    send_sem=b_send_sem.at[a, c, d],
                    recv_sem=b_recv_sem.at[a, c, d],
                    device_id=(peer(d), me_i),
                    device_id_type=MESH,
                ).wait_recv()
            copy = pltpu.make_async_copy(
                back.at[:, :, seg], back_hbm.at[:, :, seg], b_out_sem.at[a, c]
            )
            copy.start()
            back_outs.append(copy)

    for c in started:
        c.wait_send()
    for c in y_copies[1]:
        c.wait_send()
    for c in back_copies:
        c.wait_send()
    for a in range(2):
        for chunk in rs[a]:
            for c in chunk:
                c.wait_send()
    for i in (n_g - 2, n_g - 1):
        slot = i % 2
        dst = pl.ds(i * gw, gw)
        pltpu.make_async_copy(
            stage.at[slot, :, pl.ds(0, 128)], gate_hbm.at[dst, :], out_sem.at[0, slot]
        ).wait()
        pltpu.make_async_copy(
            stage.at[slot, :, pl.ds(128, 128)], up_hbm.at[dst, :], out_sem.at[1, slot]
        ).wait()
        pltpu.make_async_copy(
            stage_d.at[slot], down_hbm.at[:, dst], out_d_sem.at[slot]
        ).wait()
    for c in back_outs:
        c.wait()
    place_out.wait()


def shards(layer_input, out_grad, expert_ids, route_scales, w_gate, w_up, w_down):
    toks, width = layer_input.shape
    n_out = lax.axis_size("outer")
    n_in = lax.axis_size("inner")
    hidden = w_gate.shape[2]
    slots = n_out * CAP
    half, quarter = width // 2, width // 4
    any_spec = pl.BlockSpec(memory_space=pl.ANY)
    vmem = pl.BlockSpec(memory_space=pltpu.VMEM)
    dma = pltpu.SemaphoreType.DMA
    back, place, gate, up, down = pl.pallas_call(
        kernel,
        out_shape=(
            jax.ShapeDtypeStruct((n_out, PAD, width), BF),
            jax.ShapeDtypeStruct((toks, n_out * PAD), BF),
            jax.ShapeDtypeStruct((width, hidden), F32),
            jax.ShapeDtypeStruct((width, hidden), F32),
            jax.ShapeDtypeStruct((hidden, width), F32),
        ),
        in_specs=[vmem, vmem] + [any_spec] * 5,
        out_specs=(any_spec,) * 5,
        scratch_shapes=[
            pltpu.VMEM((2, toks, width), BF),
            pltpu.VMEM((width, 2 * hidden), BF),
            pltpu.VMEM((hidden, width), BF),
            pltpu.VMEM((toks, n_out * PAD), BF),
            pltpu.VMEM((2, n_out, PAD, width), BF),
            pltpu.VMEM((2, n_out, PAD, width), BF),
            pltpu.VMEM((n_out, PAD, width), BF),
            pltpu.VMEM((2, n_in, slots, width), BF),
            pltpu.VMEM((n_in, slots, 2 * hidden), F32),
            pltpu.VMEM((n_in, slots, hidden), F32),
            pltpu.VMEM((n_in, slots, 2 * hidden), BF),
            pltpu.VMEM((n_in, slots, hidden), BF),
            pltpu.VMEM((2, 2, 2, slots, half), BF),
            pltpu.VMEM((2, 2, 2, slots, half), BF),
            pltpu.VMEM((2, 2, SIDE, slots, half), BF),
            pltpu.VMEM((2, 2, SIDE, slots, half), BF),
            pltpu.VMEM((2, SIDE, slots, half), BF),
            pltpu.VMEM((2, 2, slots, quarter), BF),
            pltpu.VMEM((2, 2, slots, half), BF),
            pltpu.VMEM((2, 512, 2 * hidden), F32),
            pltpu.VMEM((2, hidden, 512), F32),
            dma((5,)),
            dma((2, 2, n_out)),
            dma((2, 2, n_out)),
            dma((2, 2, n_out)),
            dma((2, 2, n_out)),
            dma((2, 20, 2)),
            dma((2, 20, 2)),
            dma((2, 2, 12)),
            dma((2, 2, 12)),
            dma((2, 2)),
            dma((2,)),
            dma((2, 2)),
            dma,
        ],
        compiler_params=pltpu.CompilerParams(
            collective_id=0, has_side_effects=True, vmem_limit_bytes=67043328
        ),
        name="expert_backward",
    )(expert_ids.T, route_scales.T, layer_input, out_grad, w_gate[0], w_up[0], w_down[0])
    in_grad = dot(place, back.reshape(n_out * PAD, width), NN).astype(BF)
    return in_grad, gate[None], up[None], down[None]


def solution(mesh):
    return jax.shard_map(
        shards,
        mesh=mesh,
        in_specs=(
            P(("outer", "inner"), None),
            P(("outer", "inner"), None),
            P(("outer", "inner"), None),
            P(("outer", "inner"), None),
            P("outer", None, "inner"),
            P("outer", None, "inner"),
            P("outer", "inner", None),
        ),
        out_specs=(
            P(("outer", "inner"), None),
            P("outer", None, "inner"),
            P("outer", None, "inner"),
            P("outer", "inner", None),
        ),
        check_vma=False,
    )
```

time: 235 us -> 222 us (0.945)
  Pallas kernels: 219 us -> 209 us
  local copies, waits for them, and re-layouts: 14.4 us -> 9.46 us
  matrix products: 0 us -> 3.05 us
    pallas_call x1, Pallas kernels: 219 us -> 209 us  [shards(): pl.pallas_call(kernel, out_shape=(jax.ShapeDtypeStruct((n_out, PAD, width...]
    unnamed x12 -> x7, local copies, waits for them, and re-layouts: 14.4 us -> 9.46 us
    dot_general x0 -> x1, matrix products: none -> 3.05 us  [dot(): return lax.dot_general(a, b, dims, preferred_element_type=F32)]
where the time goes in v2:
time: 222 us
  Pallas kernels  209 us (94%)
  local copies, waits for them, and re-layouts  9.46 us (4%)
  matrix products  3.05 us (1%)
    pallas_call x1, Pallas kernels, shards(): pl.pallas_call(kernel, out_shape=(jax.ShapeDtypeStruct((n_out, PAD, width...  209 us
    unnamed x7, local copies, waits for them, and re-layouts  9.46 us

profile of v2, /device:TPU:1, one launch (start us, length us, event | category | flops | bytes accessed | tf_op | source)
XLA Modules:
  0.0 222.3 jit_solution(2901531194786493811)
XLA Ops:
  0.6 209.1 %expert_backward.1 = (bf16[8,8,7168]{2,1,0:T(8,128)(2,1)}, bf16[128,64]{1,0:T(8,128)(2,1)}, f32[7168,128]{1,0:T(8,128)}, f32[7168,128]{1,0:T(8,128)}, f32[128,7168]{1,0:T(8,128)}) custom-call(s32[8,128]{1,0:T(8,128)} %bitcast.18, f32[8,128]{1,0:T(8,128)} %bitcast.19, bf16[128,7168]{1,0:T(8,128)(2,1)} %x_hbm.1, bf16[128,7168]{1,0:T(8,128)(2,1)} %dy_hbm.1, ...), custom_call_target="tpu_custom_call" | custom-call | tf_op jit(solution)/shard_map/expert_backward/pallas_call | solution.py:582
  209.8 3.1 %convolution_convert_fusion = bf16[128,7168]{1,0:T(8,128)(2,1)} fusion(bf16[128,64]{1,0:T(8,128)(2,1)} %get-tuple-element.9, bf16[8,8,7168]{2,1,0:T(8,128)(2,1)} %get-tuple-element.10), kind=kOutput, calls=%fused_computation | convolution fusion | flops 118358016 | bytes 2768896 | tf_op jit(solution)/shard_map/dot_general | solution.py:20
  212.8 0.0 copy-start.1
  212.8 4.3 %copy.14 = f32[1,7168,128]{2,1,0:T(8,128)} copy(f32[1,7168,128]{2,1,0:T(8,128)} %bitcast.14) | data formatting | bytes 7340032
  217.1 0.0 copy-done.1
  217.1 0.0 copy-start
  217.1 1.9 copy.15
  219.0 1.5 copy-done
  220.5 1.8 copy.16
Async XLA Ops:
  212.8 4.3 %copy-start.1 = (f32[7168,128]{1,0:T(8,128)S(1)}, f32[7168,128]{1,0:T(8,128)}, u32[]{:S(2)}) copy-start(f32[7168,128]{1,0:T(8,128)} %get-tuple-element.12) | copy-start | bytes 11010052
  217.1 3.4 %copy-start = (f32[128,7168]{1,0:T(8,128)S(1)}, f32[128,7168]{1,0:T(8,128)}, u32[]{:S(2)}) copy-start(f32[128,7168]{1,0:T(8,128)} %get-tuple-element.13) | copy-start | bytes 11010052

commit v3 on v2

--- a/solution.py
+++ b/solution.py
@@ -68,7 +68,7 @@
         pltpu.make_async_copy(wu_hbm, wgu.at[:, pl.ds(128, 128)], load_sem.at[3]),
         pltpu.make_async_copy(wd_hbm, wd, load_sem.at[4]),
     ]
-    for c in loads:
+    for c in loads[:2]:
         c.start()
 
     ids = jnp.transpose(ids_ref[...].astype(F32))
@@ -134,6 +134,9 @@
     y_copies = [[], []]
     for a in range(2):
         loads[a].wait()
+        if a == 1:
+            for c in loads[2:]:
+                c.start()
         for h in range(2):
             pick(a, h)
             if a == 0 and h == 0:
@@ -242,6 +245,8 @@
         ag_wait(a, 2, ring(f, 2), s, 0)
         ag_wait(a, 3, ring(f, 2), s, 1)
         out_second(a, 2)
+
+    def round2_on(a):
         for off in (3, 1):
             on_second_plus(a, off)
             on_second_minus(a, off)
@@ -280,6 +285,8 @@
         forward(a, [(1, 0), (3, 0), (0, 1), (0, 3)])
     round2(0)
     round2(1)
+    round2_on(0)
+    round2_on(1)
     for a in range(2):
         on_second_far(a, 0)
         forward(a, [(2, 0), (1, 1), (3, 1), (1, 3), (3, 3), (0, 2)])

time: 222 us -> 223 us (level)
  no operation moved by 1% of the time
where the time goes in v3:
time: 223 us; the launch traced here: 222 us
  Pallas kernels  209 us (94%)
  local copies, waits for them, and re-layouts  9.46 us (4%)
  matrix products  3.05 us (1%)
    pallas_call x1, Pallas kernels, shards(): pl.pallas_call(kernel, out_shape=(jax.ShapeDtypeStruct((n_out, PAD, width...  209 us
    unnamed x7, local copies, waits for them, and re-layouts  9.46 us

profile of v3, /device:TPU:1, one launch (start us, length us, event | category | flops | bytes accessed | tf_op | source)
XLA Modules:
  0.0 222.3 jit_solution(13778444117071955318)
XLA Ops:
  0.6 209.1 %expert_backward.1 = (bf16[8,8,7168]{2,1,0:T(8,128)(2,1)}, bf16[128,64]{1,0:T(8,128)(2,1)}, f32[7168,128]{1,0:T(8,128)}, f32[7168,128]{1,0:T(8,128)}, f32[128,7168]{1,0:T(8,128)}) custom-call(s32[8,128]{1,0:T(8,128)} %bitcast.18, f32[8,128]{1,0:T(8,128)} %bitcast.19, bf16[128,7168]{1,0:T(8,128)(2,1)} %x_hbm.1, bf16[128,7168]{1,0:T(8,128)(2,1)} %dy_hbm.1, ...), custom_call_target="tpu_custom_call" | custom-call | tf_op jit(solution)/shard_map/expert_backward/pallas_call | solution.py:589
  209.8 3.0 %convolution_convert_fusion = bf16[128,7168]{1,0:T(8,128)(2,1)} fusion(bf16[128,64]{1,0:T(8,128)(2,1)} %get-tuple-element.9, bf16[8,8,7168]{2,1,0:T(8,128)(2,1)} %get-tuple-element.10), kind=kOutput, calls=%fused_computation | convolution fusion | flops 118358016 | bytes 2768896 | tf_op jit(solution)/shard_map/dot_general | solution.py:20
  212.8 0.0 copy-start.1
  212.8 4.3 %copy.14 = f32[1,7168,128]{2,1,0:T(8,128)} copy(f32[1,7168,128]{2,1,0:T(8,128)} %bitcast.14) | data formatting | bytes 7340032
  217.1 0.0 copy-done.1
  217.1 0.0 copy-start
  217.1 1.9 copy.15
  219.0 1.5 copy-done
  220.5 1.8 copy.16
Async XLA Ops:
  212.8 4.3 %copy-start.1 = (f32[7168,128]{1,0:T(8,128)S(1)}, f32[7168,128]{1,0:T(8,128)}, u32[]{:S(2)}) copy-start(f32[7168,128]{1,0:T(8,128)} %get-tuple-element.12) | copy-start | bytes 11010052
  217.1 3.4 %copy-start = (f32[128,7168]{1,0:T(8,128)S(1)}, f32[128,7168]{1,0:T(8,128)}, u32[]{:S(2)}) copy-start(f32[128,7168]{1,0:T(8,128)} %get-tuple-element.13) | copy-start | bytes 11010052

commit v4 on v3

--- a/solution.py
+++ b/solution.py
@@ -256,20 +256,24 @@
         on_second_minus(a, 2)
 
     def forward(a, blocks):
-        for off_f, off_s in blocks:
-            b = block(a, ring(first[a], off_f), ring(second[a], off_s))
-            if a == 0:
-
-                def step(j, acc, b=b):
-                    return acc + dot(rows[0, b, :, span(j)], wgu[span(j), :], NN)
-
-                gu[b] = lax.fori_loop(0, n_c, step, jnp.zeros((slots, 256), F32))
-            else:
-
-                def step(j, acc, b=b):
-                    return acc + dot(rows[1, b, :, span(j)], wd[:, span(j)], NT)
-
-                hid[b] = lax.fori_loop(0, n_c, step, jnp.zeros((slots, 128), F32))
+        size = 3 if len(blocks) == 6 else 4
+        for start in range(0, len(blocks), size):
+            bs = [
+                block(a, ring(first[a], off_f), ring(second[a], off_s))
+                for off_f, off_s in blocks[start : start + size]
+            ]
+
+            def step(j, acc, bs=bs):
+                m = jnp.concatenate([rows[a, b, :, span(j)] for b in bs], axis=0)
+                if a == 0:
+                    return acc + dot(m, wgu[span(j), :], NN)
+                return acc + dot(m, wd[:, span(j)], NT)
+
+            out = gu if a == 0 else hid
+            acc = jnp.zeros((len(bs) * slots, out.shape[2]), F32)
+            acc = lax.fori_loop(0, n_c, step, acc)
+            for n, b in enumerate(bs):
+                out[b] = acc[n * slots : (n + 1) * slots]
 
     for a in range(2):
         for h in range(2):

time: 223 us -> 216 us (0.969)
  Pallas kernels: 209 us -> 203 us
    pallas_call x1, Pallas kernels: 209 us -> 203 us  [shards(): pl.pallas_call(kernel, out_shape=(jax.ShapeDtypeStruct((n_out, PAD, width...]
where the time goes in v4:
time: 216 us
  Pallas kernels  203 us (94%)
  local copies, waits for them, and re-layouts  9.46 us (4%)
  matrix products  3.05 us (1%)
    pallas_call x1, Pallas kernels, shards(): pl.pallas_call(kernel, out_shape=(jax.ShapeDtypeStruct((n_out, PAD, width...  203 us
    unnamed x7, local copies, waits for them, and re-layouts  9.46 us

profile of v4, /device:TPU:1, one launch (start us, length us, event | category | flops | bytes accessed | tf_op | source)
XLA Modules:
  0.0 216.2 jit_solution(12533163077195679233)
XLA Ops:
  0.6 203.1 %expert_backward.1 = (bf16[8,8,7168]{2,1,0:T(8,128)(2,1)}, bf16[128,64]{1,0:T(8,128)(2,1)}, f32[7168,128]{1,0:T(8,128)}, f32[7168,128]{1,0:T(8,128)}, f32[128,7168]{1,0:T(8,128)}) custom-call(s32[8,128]{1,0:T(8,128)} %bitcast.18, f32[8,128]{1,0:T(8,128)} %bitcast.19, bf16[128,7168]{1,0:T(8,128)(2,1)} %x_hbm.1, bf16[128,7168]{1,0:T(8,128)(2,1)} %dy_hbm.1, ...), custom_call_target="tpu_custom_call" | custom-call | tf_op jit(solution)/shard_map/expert_backward/pallas_call | solution.py:593
  203.7 3.0 %convolution_convert_fusion = bf16[128,7168]{1,0:T(8,128)(2,1)} fusion(bf16[128,64]{1,0:T(8,128)(2,1)} %get-tuple-element.9, bf16[8,8,7168]{2,1,0:T(8,128)(2,1)} %get-tuple-element.10), kind=kOutput, calls=%fused_computation | convolution fusion | flops 118358016 | bytes 2768896 | tf_op jit(solution)/shard_map/dot_general | solution.py:20
  206.7 0.0 copy-start.1
  206.7 4.3 %copy.14 = f32[1,7168,128]{2,1,0:T(8,128)} copy(f32[1,7168,128]{2,1,0:T(8,128)} %bitcast.14) | data formatting | bytes 7340032
  211.0 0.0 copy-done.1
  211.0 0.0 copy-start
  211.0 1.9 copy.15
  212.9 1.5 copy-done
  214.4 1.8 copy.16
Async XLA Ops:
  206.7 4.3 %copy-start.1 = (f32[7168,128]{1,0:T(8,128)S(1)}, f32[7168,128]{1,0:T(8,128)}, u32[]{:S(2)}) copy-start(f32[7168,128]{1,0:T(8,128)} %get-tuple-element.12) | copy-start | bytes 11010052
  211.0 3.4 %copy-start = (f32[128,7168]{1,0:T(8,128)S(1)}, f32[128,7168]{1,0:T(8,128)}, u32[]{:S(2)}) copy-start(f32[128,7168]{1,0:T(8,128)} %get-tuple-element.13) | copy-start | bytes 11010052
